TPU v7x, 32 devices: a whole 2x2x4 slice. The times are simulated.
32 devices in a mesh: dp: 4 (over z), group: 8 (over y, x, core).
Axes of the slice: x: 2, y: 2, z: 4, core: 2. Of those that a mesh axis runs over, the one named last changes fastest.
Arguments:
- query: bfloat16 [4096, 4096], P(('dp', 'group')), may hold values from -6 to 6
- comp_key: bfloat16 [4096, 512], P(('dp', 'group')), may hold values from -6 to 6
- comp_value: bfloat16 [4096, 512], P(('dp', 'group')), may hold values from -6 to 6
- prompt_key: bfloat16 [128, 512], P(('dp', 'group')), may hold values from -6 to 6
- prompt_value: bfloat16 [128, 512], P(('dp', 'group')), may hold values from -6 to 6
- d_out: bfloat16 [4096, 4096], P(('dp', 'group')), may hold values from -6 to 6
- q_gain: float32 [128], replicated, may hold values from 0.5 to 1.5
- k_gain: float32 [128], replicated, may hold values from 0.5 to 1.5
- lengths: int32 [32], P(('dp', 'group')), may hold values from 1 to 128, 2560 in all
Outputs:
- d_query: bfloat16 [4096, 4096], P(('dp', 'group'))
- d_comp_key: bfloat16 [4096, 512], P(('dp', 'group'))
- d_comp_value: bfloat16 [4096, 512], P(('dp', 'group'))
- d_prompt_key: bfloat16 [128, 512], P(('dp', 'group'))
- d_prompt_value: bfloat16 [128, 512], P(('dp', 'group'))
- d_q_gain: float32 [128], replicated
- d_k_gain: float32 [128], replicated
Inputs may be any that keep to these rules, and one draw needn't show every extreme that they name: `lengths`: each entry is the live slots of one completion, at most 128; some completion has exactly 128.
All inputs are finite; a program needn't handle non-finite values. No bound on the sum of `lengths` on one device may be relied on, other than what follows from the above.
Results may differ from a plain program's by a relative error of at most 0.025.
Values may be sent and summed in bfloat16 or wider, within the bound.
A program may use at most 64 MiB of HBM per device.

v0:
```python
import jax
import jax.numpy as jnp
from jax import lax
from jax.sharding import PartitionSpec as P

HD = 128
HQ = 32
HK = 4
EPS = 1e-06


def normalize(vectors, gain):
    wide = vectors.astype(jnp.float32)
    inverse = lax.rsqrt(jnp.mean(wide * wide, axis=-1, keepdims=True) + EPS)
    unit = wide * inverse
    return ((unit * gain).astype(jnp.bfloat16), unit, inverse)


def norm_back(grad, unit, inverse, gain):
    scaled = grad * gain
    back = inverse * (scaled - unit * jnp.mean(scaled * unit, axis=-1, keepdims=True))
    return (back, jnp.sum((grad * unit).reshape(-1, unit.shape[-1]), axis=0))


def head_grads(query_head, key_head, value_head, grad_head, visible, scale):
    scores = (
        jnp.einsum("cgd,kd->gck", query_head, key_head, preferred_element_type=jnp.float32) * scale
    )
    expo = jnp.where(visible[None], jnp.exp(scores), 0.0)
    totals = jnp.sum(expo, axis=-1, keepdims=True)
    rounded = (expo / totals).astype(jnp.bfloat16)
    output = jnp.einsum("gck,kd->cgd", rounded, value_head, preferred_element_type=jnp.float32)
    delta = jnp.transpose(jnp.sum(grad_head.astype(jnp.float32) * output, axis=-1))[..., None]
    dprob = jnp.einsum("cgd,kd->gck", grad_head, value_head, preferred_element_type=jnp.float32)
    dscore = (expo / totals * (dprob - delta)).astype(jnp.bfloat16)
    dquery = jnp.einsum("gck,kd->cgd", dscore, key_head, preferred_element_type=jnp.float32) * scale
    dkey = jnp.einsum("gck,cgd->kd", dscore, query_head, preferred_element_type=jnp.float32) * scale
    dvalue = jnp.einsum("gck,cgd->kd", rounded, grad_head, preferred_element_type=jnp.float32)
    return (dquery, dkey, dvalue, totals, delta)


def local(query, comp_key, comp_value, prompt_key, prompt_value, d_out, q_gain, k_gain, lengths):
    count = query.shape[0]
    shard = prompt_key.shape[0]
    groups = HQ // HK
    scale = HD ** (-0.5)
    qnorm, qunit, qinv = normalize(query.reshape(count, HQ, HD), q_gain)
    cnorm, cunit, cinv = normalize(comp_key.reshape(count, HK, HD), k_gain)
    pnorm, punit, pinv = normalize(prompt_key.reshape(shard, HK, HD), k_gain)
    pkeys, pvalues = (
        lax.all_gather(pnorm.reshape(shard, HK * HD), "group", axis=0, tiled=True),
        lax.all_gather(prompt_value, "group", axis=0, tiled=True),
    )
    prompt_len = pkeys.shape[0]
    keys = jnp.concatenate([pkeys, cnorm.reshape(count, HK * HD)], axis=0).reshape(-1, HK, HD)
    values = jnp.concatenate([pvalues, comp_value], axis=0).reshape(-1, HK, HD)
    slots = lax.broadcasted_iota(jnp.int32, (count, count), 0)
    others = lax.broadcasted_iota(jnp.int32, (count, count), 1)
    visible = jnp.concatenate([jnp.ones((count, prompt_len), bool), others <= slots], axis=1)
    live = (jnp.arange(count, dtype=jnp.int32) < lengths[0])[:, None]
    masked = jnp.where(live, d_out, jnp.zeros_like(d_out))
    query_four = qnorm.reshape(count, HK, groups, HD)
    grad_four = masked.reshape(count, HK, groups, HD)
    results = [
        head_grads(
            query_four[:, head], keys[:, head], values[:, head], grad_four[:, head], visible, scale
        )
        for head in range(HK)
    ]
    dquery = jnp.stack([item[0] for item in results], axis=1).reshape(count, HQ, HD)
    dkey_all = jnp.stack([item[1] for item in results], axis=1)
    dvalue_all = jnp.stack([item[2] for item in results], axis=1)
    term = jnp.concatenate(
        [
            dkey_all[:prompt_len].reshape(prompt_len, HK * HD),
            dvalue_all[:prompt_len].reshape(prompt_len, HK * HD),
        ],
        axis=1,
    )
    summed = lax.psum_scatter(
        term.astype(jnp.bfloat16), "group", scatter_dimension=0, tiled=True
    ).astype(jnp.float32)
    dkey_comp = dkey_all[prompt_len:]
    dvalue_comp = dvalue_all[prompt_len:]
    dkey_prompt = summed[:, : HK * HD].reshape(shard, HK, HD)
    dvalue_prompt = summed[:, HK * HD :]
    dq, gain_query = norm_back(dquery, qunit, qinv, q_gain)
    dck, gain_comp = norm_back(dkey_comp, cunit, cinv, k_gain)
    dpk, gain_prompt = norm_back(dkey_prompt, punit, pinv, k_gain)
    gain_query, gain_key = lax.psum((gain_query, gain_comp + gain_prompt), ("dp", "group"))
    return (
        dq.reshape(count, HQ * HD).astype(jnp.bfloat16),
        dck.reshape(count, HK * HD).astype(jnp.bfloat16),
        dvalue_comp.reshape(count, HK * HD).astype(jnp.bfloat16),
        dpk.reshape(shard, HK * HD).astype(jnp.bfloat16),
        dvalue_prompt.astype(jnp.bfloat16),
        gain_query,
        gain_key,
    )


def solution(mesh):
    return jax.shard_map(
        local,
        mesh=mesh,
        in_specs=(
            P(("dp", "group"), None),
            P(("dp", "group"), None),
            P(("dp", "group"), None),
            P(("dp", "group"), None),
            P(("dp", "group"), None),
            P(("dp", "group"), None),
            P(),
            P(),
            P(("dp", "group")),
        ),
        out_specs=(
            P(("dp", "group"), None),
            P(("dp", "group"), None),
            P(("dp", "group"), None),
            P(("dp", "group"), None),
            P(("dp", "group"), None),
            P(),
            P(),
        ),
        check_vma=False,
    )
```

profile of v0, /device:TPU:0, one launch (start us, length us, event | category | flops | bytes accessed | tf_op | source)
XLA Modules:
  0.0 174.6 jit_solution(7659037354188881462)
XLA Ops:
  7.2 0.6 iota_compare_fusion
  7.8 0.7 broadcast_bitcast_fusion.3
  8.5 0.7 reshape.176
  9.9 0.6 copy-done.32
  10.5 0.7 fusion.87
  11.2 10.6 %all-gather = bf16[8,4,512]{2,1,0:T(4,128)(2,1)S(1)} all-gather(bf16[1,4,512]{2,1,0:T(4,128)(2,1)S(1)} %fusion.87), channel_id=1, replica_groups=mesh['dp'=4,'group'=8] {'group'}, dimensions={0}, use_global_device_ids=true | all-gather | bytes 36864 | tf_op jit(solution)/shard_map/all_gather | solution.py:51
  21.8 0.6 copy.94
  22.4 1.0 copy.92
  23.8 0.7 copy.91
  24.7 0.8 add_rsqrt_fusion
  26.0 1.3 concatenate.21
  27.3 1.3 fusion.81
  28.6 1.4 multiply_convert_fusion
  30.0 2.0 %fusion.52 = f32[8,128,160]{1,2,0:T(8,128)} fusion(pred[128,160]{0,1:T(8,128)(4,1)} %concatenate.21, bf16[128,4,8,128]{3,0,2,1:T(8,128)(2,1)S(1)} %multiply_convert_fusion, bf16[128,4,128]{2,0,1:T(8,128)(2,1)S(1)} %copy.95, bf16[32,4,128]{2,0,1:T(8,128)(2,1)} %copy.94), kind=kOutput, calls=%fused_computation.88 | convolution fusion | flops 42517664 | bytes 1101824 | tf_op jit(solution)/shard_map/div | solution.py:35
  32.0 1.9 %fusion.54 = f32[8,128,160]{1,2,0:T(8,128)} fusion(pred[128,160]{0,1:T(8,128)(4,1)} %concatenate.21, bf16[128,4,8,128]{3,0,2,1:T(8,128)(2,1)S(1)} %multiply_convert_fusion, bf16[128,4,128]{2,0,1:T(8,128)(2,1)S(1)} %copy.95, bf16[32,4,128]{2,0,1:T(8,128)(2,1)} %copy.94), kind=kOutput, calls=%fused_computation.90 | convolution fusion | flops 42517664 | bytes 1101824 | tf_op jit(solution)/shard_map/div | solution.py:35
  33.9 2.0 %fusion.56 = f32[8,128,160]{1,2,0:T(8,128)} fusion(pred[128,160]{0,1:T(8,128)(4,1)} %concatenate.21, bf16[128,4,8,128]{3,0,2,1:T(8,128)(2,1)S(1)} %multiply_convert_fusion, bf16[128,4,128]{2,0,1:T(8,128)(2,1)S(1)} %copy.95, bf16[32,4,128]{2,0,1:T(8,128)(2,1)} %copy.94), kind=kOutput, calls=%fused_computation.92 | convolution fusion | flops 42517664 | bytes 1101824 | tf_op jit(solution)/shard_map/div | solution.py:35
  37.1 9.3 %all-gather.1 = bf16[8,4,512]{2,1,0:T(4,128)(2,1)S(1)} all-gather(bf16[1,4,512]{2,1,0:T(4,128)(2,1)} %bitcast.375), channel_id=1, replica_groups=mesh['dp'=4,'group'=8] {'group'}, dimensions={0}, use_global_device_ids=true | all-gather | bytes 36864 | tf_op jit(solution)/shard_map/all_gather | solution.py:52
  46.3 0.9 pad_maximum_fusion.2
  47.3 0.9 fusion.122
  48.2 2.3 %copy.98 = bf16[128,4096]{0,1:T(8,128)(2,1)} copy(bf16[128,4096]{1,0:T(8,128)(2,1)} %param.14) | data formatting | bytes 2097152 | tf_op args[5]
  50.5 1.3 broadcast_select_fusion
  51.8 1.0 fusion.121
  52.8 1.8 %copy.133 = bf16[128,1,8,128]{3,0,2,1:T(8,128)(2,1)} copy(bf16[128,1,8,128]{0,3,2,1:T(8,128)(2,1)} %get-tuple-element.38) | data formatting | bytes 524288
  54.6 1.8 %copy.137 = bf16[128,1,8,128]{3,0,2,1:T(8,128)(2,1)} copy(bf16[128,1,8,128]{0,3,2,1:T(8,128)(2,1)} %get-tuple-element.39) | data formatting | bytes 524288
  56.4 1.8 %copy.135 = bf16[128,1,8,128]{3,0,2,1:T(8,128)(2,1)} copy(bf16[128,1,8,128]{0,3,2,1:T(8,128)(2,1)} %get-tuple-element.40) | data formatting | bytes 524288
  58.2 1.8 %copy.139 = bf16[128,1,8,128]{3,0,2,1:T(8,128)(2,1)} copy(bf16[128,1,8,128]{0,3,2,1:T(8,128)(2,1)} %get-tuple-element.41) | data formatting | bytes 524288
  60.0 2.1 %fusion.50 = f32[8,128,160]{1,2,0:T(8,128)} fusion(bf16[160,128,1]{1,0,2:T(8,128)(2,1)} %fusion.81, pred[128,160]{0,1:T(8,128)(4,1)} %concatenate.21, bf16[128,4,8,128]{3,0,2,1:T(8,128)(2,1)} %copy-done.6), kind=kOutput, calls=%fused_computation.86 | convolution fusion | flops 42435744 | bytes 978944 | tf_op jit(solution)/shard_map/div | solution.py:35
  62.1 1.5 convolution_bitcast_fusion.8
  63.6 1.7 fusion.37
  65.3 1.1 fusion.36
  71.2 0.6 pad_maximum_fusion.3
  71.9 1.3 broadcast_bitcast_fusion
  73.2 2.1 %fusion.29 = f32[128,1,8,128]{3,0,2,1:T(8,128)} fusion(bf16[160,128,1]{1,0,2:T(8,128)(2,1)} %fusion.81, bf16[8,128,160]{1,2,0:T(8,128)(2,1)} %copy-done.8), kind=kOutput, calls=%fused_computation.51 | convolution fusion | flops 42074112 | bytes 892928 | tf_op jit(solution)/shard_map/gck,kd->cgd/dot_general | solution.py:36
  75.3 2.2 %fusion.30 = f32[128,1,8,128]{3,0,2,1:T(8,128)} fusion(bf16[8,128,160]{1,2,0:T(8,128)(2,1)} %copy-done.9, bf16[128,4,128]{2,0,1:T(8,128)(2,1)S(1)} %copy.95, bf16[32,4,128]{2,0,1:T(8,128)(2,1)} %copy.94), kind=kOutput, calls=%fused_computation.53 | convolution fusion | flops 42156032 | bytes 1015808 | tf_op jit(solution)/shard_map/gck,kd->cgd/dot_general | solution.py:36
  77.5 1.2 fusion.31
  78.7 0.7 maximum_convert_fusion
  79.4 1.1 fusion.32
  81.2 3.6 %multiply_reduce_fusion = (f32[128,4,8]{0,2,1:T(8,128)S(1)}, f32[128,4,8,128]{3,0,2,1:T(8,128)}) fusion(f32[128,4,8,128]{3,0,2,1:T(8,128)S(1)} %copy.96, f32[128]{0:T(128)S(1)} %copy-done.45, f32[128,4,8]{0,2,1:T(8,128)S(1)} %get-tuple-element.49, f32[128,1,8,128]{3,0,2,1:T(8,128)} %fusion.29, f32[128,1,8,128]{3,0,2,1:T(8,128)} %fusion.30, ...), kind=kLoop, calls=%fused_computation.11 | loop fusion | flops 3665920 | bytes 6324736 | tf_op jit(solution)/shard_map/reduce_sum | solution.py:21
  84.8 2.0 %copy.114 = f32[128,4,8,128]{0,3,2,1:T(8,128)S(1)} copy(f32[128,4,8,128]{3,0,2,1:T(8,128)} %get-tuple-element.37) | data formatting | bytes 4194304 | tf_op jit(solution)/shard_map/stack | solution.py:70
  86.8 2.2 %fusion.4 = (f32[4096]{0:T(1024)S(1)}, bf16[128,4096]{0,1:T(8,128)(2,1)}) fusion(f32[128,4,8,128]{0,3,2,1:T(8,128)S(1)} %copy.114, bf16[128,4096]{0,1:T(8,128)(2,1)S(1)} %copy-done.1, f32[128,4,8]{0,2,1:T(8,128)S(1)} %get-tuple-element.49, f32[128,32]{0,1:T(8,128)S(1)} %multiply_bitcast_fusion, f32[4096]{0:T(1024)S(1)} %copy-done.35, f32[128,32]{0,1:T(8,128)S(1)} %copy-done.34), kind=kLoop, calls=%fused_computation.8 | loop fusion | flops 5238784 | bytes 4276224 | tf_op jit(solution)/shard_map/reduce_sum | solution.py:22
  89.3 0.8 copy.123
  90.2 0.8 copy.122
  91.0 2.3 %copy.121 = bf16[128,4096]{1,0:T(8,128)(2,1)} copy(bf16[128,4096]{0,1:T(8,128)(2,1)} %get-tuple-element.35) | data formatting | bytes 2097152
  93.3 0.6 dynamic-slice
  94.5 30.9 %all-reduce.5.cloned.1.call-done = bf16[32,1024]{1,0:T(8,128)(2,1)} async-done(((bf16[32,1024]{1,0:T(8,128)(2,1)}), bf16[32,1024]{1,0:T(8,128)(2,1)}) %all-reduce.5.cloned.1.call-update) | async-done | bytes 65552
  125.4 1.4 fusion.123
  127.2 39.3 %all-reduce.2 = (f32[128]{0:T(128)}, f32[128]{0:T(128)}) all-reduce(f32[128]{0:T(128)S(1)} %bitcast_reduce_fusion.1, f32[128]{0:T(128)S(1)} %add.48), channel_id=1, replica_groups=mesh['dp'=4,'group'=8] {'dp','group'}, use_global_device_ids=true, to_apply=%region_17.18 | all-reduce | flops 256 | bytes 2048 | tf_op jit(solution)/shard_map/psum | solution.py:90
  166.5 1.3 fusion.86
  (142 shorter events, 8.2 us)
Async XLA Ops:
  7.2 16.6 %copy-start.14 = (bf16[128,4096]{1,0:T(8,128)(2,1)S(1)}, bf16[128,4096]{1,0:T(8,128)(2,1)}, u32[]{:S(2)}) copy-start(bf16[128,4096]{1,0:T(8,128)(2,1)} %param.9) | copy-start | bytes 3145732
  7.2 118.3 %all-reduce.5.cloned.1.call-start = ((), (), s32[]{:S(2)}) async-start(), calls=%async_computation | async-start | bytes 131072
  8.5 16.2 %copy-start.39 = (f32[512]{0:T(512)}, f32[512]{0:T(512)S(1)}, u32[]{:S(2)}) copy-start(f32[512]{0:T(512)S(1)} %broadcast_bitcast_fusion.3) | copy-start | bytes 6148
  9.2 0.6 copy-start.30
  9.9 0.6 copy-start.32
  23.5 2.0 %copy-start.37 = (f32[128,4]{0,1:T(4,128)}, f32[128,4]{0,1:T(4,128)S(1)}, u32[]{:S(2)}) copy-start(f32[128,4]{0,1:T(4,128)S(1)} %add_rsqrt_fusion.1) | copy-start | bytes 6148
  24.4 1.6 copy-start
  30.0 3.9 %copy-start.6 = (bf16[128,4,8,128]{3,0,2,1:T(8,128)(2,1)}, bf16[128,4,8,128]{3,0,2,1:T(8,128)(2,1)S(1)}, u32[]{:S(2)}) copy-start(bf16[128,4,8,128]{3,0,2,1:T(8,128)(2,1)S(1)} %multiply_convert_fusion) | copy-start | bytes 3145732
  62.1 3.2 %copy-start.5 = (f32[8,128,160]{1,2,0:T(8,128)S(1)}, f32[8,128,160]{1,2,0:T(8,128)}, u32[]{:S(2)}) copy-start(f32[8,128,160]{1,2,0:T(8,128)} %fusion.50) | copy-start | bytes 1966084
  62.1 4.4 %copy-start.7 = (bf16[128,4,8,128]{3,0,2,1:T(8,128)(2,1)S(1)}, bf16[128,4,8,128]{3,0,2,1:T(8,128)(2,1)}, u32[]{:S(2)}) copy-start(bf16[128,4,8,128]{3,0,2,1:T(8,128)(2,1)} %copy-done.6) | copy-start | bytes 3145732
  62.1 4.6 %copy-start.4 = (f32[8,128,160]{1,2,0:T(8,128)S(1)}, f32[8,128,160]{1,2,0:T(8,128)}, u32[]{:S(2)}) copy-start(f32[8,128,160]{1,2,0:T(8,128)} %fusion.52) | copy-start | bytes 1966084
  63.6 7.2 %copy-start.19 = (bf16[160,1,128]{2,0,1:T(8,128)(2,1)}, bf16[160,1,128]{2,0,1:T(8,128)(2,1)S(1)}, u32[]{:S(2)}) copy-start(bf16[160,1,128]{2,0,1:T(8,128)(2,1)S(1)} %convolution_bitcast_fusion.8) | copy-start | bytes 122884
  63.6 3.4 %copy-start.17 = (bf16[128,1,8,128]{3,0,2,1:T(8,128)(2,1)S(1)}, bf16[128,1,8,128]{3,0,2,1:T(8,128)(2,1)}, u32[]{:S(2)}) copy-start(bf16[128,1,8,128]{3,0,2,1:T(8,128)(2,1)} %copy.137) | copy-start | bytes 786436
  63.6 3.4 %copy-start.29 = (bf16[160,1,128]{2,1,0:T(2,128)(2,1)S(1)}, bf16[160,1,128]{2,1,0:T(2,128)(2,1)}, u32[]{:S(2)}) copy-start(bf16[160,1,128]{2,1,0:T(2,128)(2,1)} %get-tuple-element.43) | copy-start | bytes 122884
  66.5 1.6 copy-start.8
  66.7 1.3 copy-start.3
  67.0 3.7 %copy-start.21 = (bf16[160,1,128]{2,0,1:T(8,128)(2,1)}, bf16[160,1,128]{2,0,1:T(8,128)(2,1)S(1)}, u32[]{:S(2)}) copy-start(bf16[160,1,128]{2,0,1:T(8,128)(2,1)S(1)} %convolution_bitcast_fusion.9) | copy-start | bytes 122884
  67.0 1.4 copy-start.16
  67.0 1.4 copy-start.28
  67.8 1.6 copy-start.9
  68.1 1.3 copy-start.2
  68.3 2.4 %copy-start.23 = (bf16[160,1,128]{2,0,1:T(8,128)(2,1)}, bf16[160,1,128]{2,0,1:T(8,128)(2,1)S(1)}, u32[]{:S(2)}) copy-start(bf16[160,1,128]{2,0,1:T(8,128)(2,1)S(1)} %convolution_bitcast_fusion.10) | copy-start | bytes 122884
  68.3 1.3 copy-start.15
  68.4 1.3 copy-start.27
  69.1 1.6 copy-start.10
  69.7 1.5 copy-start.25
  70.4 0.7 copy-start.12
  70.4 7.1 %copy-start.18 = (bf16[32,4,128]{2,0,1:T(8,128)(2,1)S(1)}, bf16[32,4,128]{2,0,1:T(8,128)(2,1)}, u32[]{:S(2)}) copy-start(bf16[32,4,128]{2,0,1:T(8,128)(2,1)} %copy.94) | copy-start | bytes 98308
  71.1 6.4 %copy-start.11 = (bf16[8,128,160]{1,2,0:T(8,128)(2,1)S(1)}, bf16[8,128,160]{1,2,0:T(8,128)(2,1)}, u32[]{:S(2)}) copy-start(bf16[8,128,160]{1,2,0:T(8,128)(2,1)} %copy-done.10) | copy-start | bytes 983044
  71.2 8.2 %copy-start.13 = (bf16[8,128,160]{1,2,0:T(8,128)(2,1)S(1)}, bf16[8,128,160]{1,2,0:T(8,128)(2,1)}, u32[]{:S(2)}) copy-start(bf16[8,128,160]{1,2,0:T(8,128)(2,1)} %copy-done.12) | copy-start | bytes 983044
  71.8 6.8 %copy-start.20 = (bf16[160,1,128]{2,0,1:T(8,128)(2,1)S(1)}, bf16[160,1,128]{2,0,1:T(8,128)(2,1)}, u32[]{:S(2)}) copy-start(bf16[160,1,128]{2,0,1:T(8,128)(2,1)} %copy-done.19) | copy-start | bytes 122884
  71.9 6.8 %copy-start.22 = (bf16[160,1,128]{2,0,1:T(8,128)(2,1)S(1)}, bf16[160,1,128]{2,0,1:T(8,128)(2,1)}, u32[]{:S(2)}) copy-start(bf16[160,1,128]{2,0,1:T(8,128)(2,1)} %copy-done.21) | copy-start | bytes 122884
  71.9 6.8 %copy-start.24 = (bf16[160,1,128]{2,0,1:T(8,128)(2,1)S(1)}, bf16[160,1,128]{2,0,1:T(8,128)(2,1)}, u32[]{:S(2)}) copy-start(bf16[160,1,128]{2,0,1:T(8,128)(2,1)} %copy-done.23) | copy-start | bytes 122884
  71.9 6.8 %copy-start.26 = (bf16[160,1,128]{2,0,1:T(8,128)(2,1)S(1)}, bf16[160,1,128]{2,0,1:T(8,128)(2,1)}, u32[]{:S(2)}) copy-start(bf16[160,1,128]{2,0,1:T(8,128)(2,1)} %copy-done.25) | copy-start | bytes 122884
  75.3 5.3 %copy-start.38 = (f32[128,4]{0,1:T(4,128)S(1)}, f32[128,4]{0,1:T(4,128)}, u32[]{:S(2)}) copy-start(f32[128,4]{0,1:T(4,128)} %copy-done.37) | copy-start | bytes 6148
  75.3 5.3 %copy-start.43 = (f32[128]{0:T(128)S(1)}, f32[128]{0:T(128)}, u32[]{:S(2)}) copy-start(f32[128]{0:T(128)} %param.16) | copy-start | bytes 1540
  77.5 3.6 %copy-start.45 = (f32[128]{0:T(128)S(1)}, f32[128]{0:T(128)}, u32[]{:S(2)}) copy-start(f32[128]{0:T(128)} %param.15) | copy-start | bytes 1540
  84.7 2.0 %copy-start.1 = (bf16[128,4096]{0,1:T(8,128)(2,1)S(1)}, bf16[128,4096]{0,1:T(8,128)(2,1)}, u32[]{:S(2)}) copy-start(bf16[128,4096]{0,1:T(8,128)(2,1)} %copy-done) | copy-start | bytes 3145732
  84.7 2.1 %copy-start.34 = (f32[128,32]{0,1:T(8,128)S(1)}, f32[128,32]{0,1:T(8,128)}, u32[]{:S(2)}) copy-start(f32[128,32]{0,1:T(8,128)} %get-tuple-element.48) | copy-start | bytes 49156
  84.7 2.1 %copy-start.35 = (f32[4096]{0:T(1024)S(1)}, f32[4096]{0:T(1024)}, u32[]{:S(2)}) copy-start(f32[4096]{0:T(1024)} %broadcast_bitcast_fusion) | copy-start | bytes 49156
  86.8 2.3 %copy-start.42 = (f32[4,4]{1,0:T(4,128)S(1)}, f32[4,4]{1,0:T(4,128)}, u32[]{:S(2)}) copy-start(f32[4,4]{1,0:T(4,128)} %copy-done.41) | copy-start | bytes 196
  86.8 2.4 %copy-start.36 = (bf16[4,512]{1,0:T(4,128)(2,1)S(1)}, bf16[4,512]{1,0:T(4,128)(2,1)}, u32[]{:S(2)}) copy-start(bf16[4,512]{1,0:T(4,128)(2,1)} %param.12) | copy-start | bytes 12292
  86.8 2.3 %slice-start = ((bf16[160,4,128]{2,0,1:T(8,128)(2,1)}), bf16[128,4,128]{2,0,1:T(8,128)(2,1)S(1)}, s32[]{:S(2)}) async-start(bf16[160,4,128]{2,0,1:T(8,128)(2,1)} %maximum_convert_fusion), calls=%async_computation.1 | async-start | bytes 262144 | tf_op jit(solution)/shard_map/slice | solution.py:84
  89.0 4.2 %copy-start.46 = (u32[32]{0:T(128)S(1)}, u32[32]{0:T(128)}, u32[]{:S(2)}) copy-start(u32[32]{0:T(128)} %constant.31) | copy-start | bytes 388
  89.0 37.8 %copy-start.31 = (f32[4,4,128]{2,1,0:T(4,128)S(1)}, f32[4,4,128]{2,1,0:T(4,128)}, u32[]{:S(2)}) copy-start(f32[4,4,128]{2,1,0:T(4,128)} %copy-done.30) | copy-start | bytes 24580
  89.0 37.8 %copy-start.44 = (f32[128]{0:T(128)S(1)}, f32[128]{0:T(128)}, u32[]{:S(2)}) copy-start(f32[128]{0:T(128)} %param.16) | copy-start | bytes 1540
  89.0 77.5 %copy-start.33 = (f32[1,4,4,128]{3,2,1,0:T(4,128)S(1)}, f32[1,4,4,128]{3,2,1,0:T(4,128)}, u32[]{:S(2)}) copy-start(f32[1,4,4,128]{3,2,1,0:T(4,128)} %copy-done.32) | copy-start | bytes 24580
  89.0 77.5 %copy-start.40 = (f32[512]{0:T(512)S(1)}, f32[512]{0:T(512)}, u32[]{:S(2)}) copy-start(f32[512]{0:T(512)} %copy-done.39) | copy-start | bytes 6148
  (1 other events, 0.6 us)
Sparse Core Ops, SparseCore 0:
  72.0 53.4 all-reduce.4
where the time goes:
time: 176 us; the launch traced here: 175 us
  blocking collectives  59.1 us (34%)
  waiting for transfers between devices  31 us (18%)
  local copies, waits for them, and re-layouts  27.1 us (15%)
  matrix products  22.8 us (13%)
  other arithmetic  18.5 us (11%)
  between operations  16.1 us (9%)
    psum x1, blocking collectives, local(): lax.psum((gain_query, gain_comp + gain_prompt), ('dp', 'group'))  39.3 us
    unnamed x2, waiting for transfers between devices  31 us
    unnamed x108, local copies, waits for them, and re-layouts  17.3 us
    all_gather x1, blocking collectives, local(): lax.all_gather(pnorm.reshape(shard, HK * HD), 'group', axis=0, tiled=True)  10.6 us
    all_gather x1, blocking collectives, local(): lax.all_gather(prompt_value, 'group', axis=0, tiled=True)  9.25 us
    div x4, matrix products, head_grads(): dscore = (expo / totals * (dprob - delta)).astype(jnp.bfloat16)  8.01 us
    dot_general x4, matrix products, head_grads(): jnp.einsum('gck,kd->cgd', dscore, key_head, preferred_element_type=jnp.fl...  6.62 us
    reduce_sum x2, other arithmetic, norm_back(): jnp.mean(scaled * unit, axis=-1, keepdims=True)  3.73 us
  transfers between devices with their start and end apart: 1, of which 1 were waited for; matrix products, arithmetic and copies ran while one was open for 12% of the time, Pallas kernels for 0%

commit v1 on v0

--- a/solution.py
+++ b/solution.py
@@ -87,7 +87,7 @@
     dq, gain_query = norm_back(dquery, qunit, qinv, q_gain)
     dck, gain_comp = norm_back(dkey_comp, cunit, cinv, k_gain)
     dpk, gain_prompt = norm_back(dkey_prompt, punit, pinv, k_gain)
-    gain_query, gain_key = lax.psum((gain_query, gain_comp + gain_prompt), ("dp", "group"))
+    gain_query, gain_key = lax.psum(lax.psum((gain_query, gain_comp + gain_prompt), "group"), "dp")
     return (
         dq.reshape(count, HQ * HD).astype(jnp.bfloat16),
         dck.reshape(count, HK * HD).astype(jnp.bfloat16),

time: 176 us -> 160 us (0.909)
  blocking collectives: 59.1 us -> 43.8 us
    psum x1 -> x2, blocking collectives: 39.3 us -> 24 us  [the longest x1 12.2 us: local(): lax.psum(lax.psum((gain_query, gain_comp + gain_prompt), 'group'), 'dp')]
    unnamed x108 -> x104, local copies, waits for them, and re-layouts: 17.3 us -> 16.4 us
  transfers between devices with their start and end apart: 1 -> 1, of which waited for: 1 -> 1; matrix products, arithmetic and copies ran while one was open for 12% -> 14% of each run, Pallas kernels for 0% -> 0%
where the time goes in v1:
time: 160 us; the launch traced here: 159 us
  blocking collectives  43.8 us (27%)
  waiting for transfers between devices  31.1 us (19%)
  local copies, waits for them, and re-layouts  26.5 us (17%)
  matrix products  22.8 us (14%)
  other arithmetic  18.9 us (12%)
  between operations  16.1 us (10%)
    unnamed x2, waiting for transfers between devices  31.1 us
    unnamed x104, local copies, waits for them, and re-layouts  16.4 us
    psum x1, blocking collectives, local(): lax.psum(lax.psum((gain_query, gain_comp + gain_prompt), 'group'), 'dp')  12.2 us
    psum x1, blocking collectives, local(): lax.psum((gain_query, gain_comp + gain_prompt), 'group')  11.8 us
    all_gather x1, blocking collectives, local(): lax.all_gather(pnorm.reshape(shard, HK * HD), 'group', axis=0, tiled=True)  10.6 us
    all_gather x1, blocking collectives, local(): lax.all_gather(prompt_value, 'group', axis=0, tiled=True)  9.25 us
    div x4, matrix products, head_grads(): dscore = (expo / totals * (dprob - delta)).astype(jnp.bfloat16)  7.97 us
    dot_general x4, matrix products, head_grads(): jnp.einsum('gck,kd->cgd', dscore, key_head, preferred_element_type=jnp.fl...  6.63 us
  transfers between devices with their start and end apart: 1, of which 1 were waited for; matrix products, arithmetic and copies ran while one was open for 14% of the time, Pallas kernels for 0%

profile of v1, /device:TPU:0, one launch (start us, length us, event | category | flops | bytes accessed | tf_op | source)
XLA Modules:
  0.0 159.3 jit_solution(5741649933149767077)
XLA Ops:
  7.2 0.6 iota_compare_fusion
  7.8 0.7 broadcast_bitcast_fusion.3
  8.5 0.7 reshape.176
  9.9 0.6 copy-done.32
  10.5 0.7 fusion.87
  11.2 10.6 %all-gather = bf16[8,4,512]{2,1,0:T(4,128)(2,1)S(1)} all-gather(bf16[1,4,512]{2,1,0:T(4,128)(2,1)S(1)} %fusion.87), channel_id=1, replica_groups=mesh['dp'=4,'group'=8] {'group'}, dimensions={0}, use_global_device_ids=true | all-gather | bytes 36864 | tf_op jit(solution)/shard_map/all_gather | solution.py:51
  21.8 0.6 copy.94
  22.4 1.0 copy.92
  23.8 0.7 copy.91
  24.7 0.7 add_rsqrt_fusion
  26.0 1.3 concatenate.21
  27.3 1.3 fusion.81
  28.6 1.4 multiply_convert_fusion
  30.0 2.0 %fusion.52 = f32[8,128,160]{1,2,0:T(8,128)} fusion(pred[128,160]{0,1:T(8,128)(4,1)} %concatenate.21, bf16[128,4,8,128]{3,0,2,1:T(8,128)(2,1)S(1)} %multiply_convert_fusion, bf16[128,4,128]{2,0,1:T(8,128)(2,1)S(1)} %copy.95, bf16[32,4,128]{2,0,1:T(8,128)(2,1)} %copy.94), kind=kOutput, calls=%fused_computation.88 | convolution fusion | flops 42517664 | bytes 1101824 | tf_op jit(solution)/shard_map/div | solution.py:35
  32.0 1.9 %fusion.54 = f32[8,128,160]{1,2,0:T(8,128)} fusion(pred[128,160]{0,1:T(8,128)(4,1)} %concatenate.21, bf16[128,4,8,128]{3,0,2,1:T(8,128)(2,1)S(1)} %multiply_convert_fusion, bf16[128,4,128]{2,0,1:T(8,128)(2,1)S(1)} %copy.95, bf16[32,4,128]{2,0,1:T(8,128)(2,1)} %copy.94), kind=kOutput, calls=%fused_computation.90 | convolution fusion | flops 42517664 | bytes 1101824 | tf_op jit(solution)/shard_map/div | solution.py:35
  33.9 1.9 %fusion.56 = f32[8,128,160]{1,2,0:T(8,128)} fusion(pred[128,160]{0,1:T(8,128)(4,1)} %concatenate.21, bf16[128,4,8,128]{3,0,2,1:T(8,128)(2,1)S(1)} %multiply_convert_fusion, bf16[128,4,128]{2,0,1:T(8,128)(2,1)S(1)} %copy.95, bf16[32,4,128]{2,0,1:T(8,128)(2,1)} %copy.94), kind=kOutput, calls=%fused_computation.92 | convolution fusion | flops 42517664 | bytes 1101824 | tf_op jit(solution)/shard_map/div | solution.py:35
  37.0 9.3 %all-gather.1 = bf16[8,4,512]{2,1,0:T(4,128)(2,1)S(1)} all-gather(bf16[1,4,512]{2,1,0:T(4,128)(2,1)} %bitcast.375), channel_id=1, replica_groups=mesh['dp'=4,'group'=8] {'group'}, dimensions={0}, use_global_device_ids=true | all-gather | bytes 36864 | tf_op jit(solution)/shard_map/all_gather | solution.py:52
  46.3 0.9 pad_maximum_fusion.2
  47.2 0.9 fusion.122
  48.2 2.3 %copy.98 = bf16[128,4096]{0,1:T(8,128)(2,1)} copy(bf16[128,4096]{1,0:T(8,128)(2,1)} %param.14) | data formatting | bytes 2097152 | tf_op args[5]
  50.5 1.3 broadcast_select_fusion
  51.8 1.0 fusion.121
  52.8 1.8 %copy.133 = bf16[128,1,8,128]{3,0,2,1:T(8,128)(2,1)} copy(bf16[128,1,8,128]{0,3,2,1:T(8,128)(2,1)} %get-tuple-element.40) | data formatting | bytes 524288
  54.6 1.8 %copy.137 = bf16[128,1,8,128]{3,0,2,1:T(8,128)(2,1)} copy(bf16[128,1,8,128]{0,3,2,1:T(8,128)(2,1)} %get-tuple-element.41) | data formatting | bytes 524288
  56.4 1.8 %copy.135 = bf16[128,1,8,128]{3,0,2,1:T(8,128)(2,1)} copy(bf16[128,1,8,128]{0,3,2,1:T(8,128)(2,1)} %get-tuple-element.42) | data formatting | bytes 524288
  58.2 1.8 %copy.139 = bf16[128,1,8,128]{3,0,2,1:T(8,128)(2,1)} copy(bf16[128,1,8,128]{0,3,2,1:T(8,128)(2,1)} %get-tuple-element.43) | data formatting | bytes 524288
  59.9 2.1 %fusion.50 = f32[8,128,160]{1,2,0:T(8,128)} fusion(bf16[160,128,1]{1,0,2:T(8,128)(2,1)} %fusion.81, pred[128,160]{0,1:T(8,128)(4,1)} %concatenate.21, bf16[128,4,8,128]{3,0,2,1:T(8,128)(2,1)} %copy-done.6), kind=kOutput, calls=%fused_computation.86 | convolution fusion | flops 42435744 | bytes 978944 | tf_op jit(solution)/shard_map/div | solution.py:35
  62.1 1.5 convolution_bitcast_fusion.8
  63.6 1.7 %fusion.37 = f32[128,8]{0,1:T(8,128)S(1)} fusion(bf16[128,1,8,128]{3,0,2,1:T(8,128)(2,1)} %copy.139, f32[8,128,160]{1,2,0:T(8,128)} %fusion.50, bf16[160,1,128]{2,1,0:T(2,128)(2,1)} %get-tuple-element.47), kind=kOutput, calls=%fused_computation.62 | convolution fusion | flops 42499072 | bytes 962560 | tf_op jit(solution)/shard_map/gck,kd->cgd/dot_general | solution.py:32
  65.3 1.1 fusion.36
  71.1 0.6 pad_maximum_fusion.3
  71.8 0.7 broadcast_bitcast_fusion
  72.5 2.1 %fusion.29 = f32[128,1,8,128]{3,0,2,1:T(8,128)} fusion(bf16[160,128,1]{1,0,2:T(8,128)(2,1)} %fusion.81, bf16[8,128,160]{1,2,0:T(8,128)(2,1)} %copy-done.8), kind=kOutput, calls=%fused_computation.51 | convolution fusion | flops 42074112 | bytes 892928 | tf_op jit(solution)/shard_map/gck,kd->cgd/dot_general | solution.py:36
  74.7 2.2 %fusion.30 = f32[128,1,8,128]{3,0,2,1:T(8,128)} fusion(bf16[8,128,160]{1,2,0:T(8,128)(2,1)} %copy-done.9, bf16[128,4,128]{2,0,1:T(8,128)(2,1)S(1)} %copy.95, bf16[32,4,128]{2,0,1:T(8,128)(2,1)} %copy.94), kind=kOutput, calls=%fused_computation.53 | convolution fusion | flops 42156032 | bytes 1015808 | tf_op jit(solution)/shard_map/gck,kd->cgd/dot_general | solution.py:36
  76.9 1.2 fusion.31
  78.1 0.7 maximum_convert_fusion
  78.7 1.1 fusion.32
  80.5 3.5 %multiply_reduce_fusion = (f32[128,4,8]{0,2,1:T(8,128)S(1)}, f32[128,4,8,128]{3,0,2,1:T(8,128)}) fusion(f32[128,4,8,128]{3,0,2,1:T(8,128)S(1)} %copy.96, f32[128]{0:T(128)S(1)} %copy-done.43, f32[128,4,8]{0,2,1:T(8,128)S(1)} %get-tuple-element.51, f32[128,1,8,128]{3,0,2,1:T(8,128)} %fusion.29, f32[128,1,8,128]{3,0,2,1:T(8,128)} %fusion.30, ...), kind=kLoop, calls=%fused_computation.11 | loop fusion | flops 3665920 | bytes 6324736 | tf_op jit(solution)/shard_map/reduce_sum | solution.py:21
  84.1 3.0 %copy.114 = f32[128,4,8,128]{0,3,2,1:T(8,128)} copy(f32[128,4,8,128]{3,0,2,1:T(8,128)} %get-tuple-element.39) | data formatting | bytes 4194304 | tf_op jit(solution)/shard_map/stack | solution.py:70
  87.1 2.6 %fusion.4 = (f32[4096]{0:T(1024)S(1)}, bf16[128,4096]{0,1:T(8,128)(2,1)S(1)}) fusion(f32[128,4,8,128]{0,3,2,1:T(8,128)} %copy.114, bf16[128,4096]{0,1:T(8,128)(2,1)S(1)} %copy-done.1, f32[128,4,8]{0,2,1:T(8,128)S(1)} %get-tuple-element.51, f32[128,32]{0,1:T(8,128)S(1)} %multiply_bitcast_fusion, f32[4096]{0:T(1024)S(1)} %broadcast_bitcast_fusion, ...), kind=kLoop, calls=%fused_computation.8 | loop fusion | flops 5238784 | bytes 4276224 | tf_op jit(solution)/shard_map/reduce_sum | solution.py:22
  90.0 0.8 copy.123
  91.0 0.8 copy.122
  91.7 1.3 copy.121
  94.3 31.1 %all-reduce.6.cloned.1.call-done = bf16[32,1024]{1,0:T(8,128)(2,1)} async-done(((bf16[32,1024]{1,0:T(8,128)(2,1)}), bf16[32,1024]{1,0:T(8,128)(2,1)}) %all-reduce.6.cloned.1.call-update) | async-done | bytes 65552
  125.4 1.4 fusion.123
  127.1 11.8 %all-reduce.2 = (f32[128]{0:T(128)S(1)}, f32[128]{0:T(128)S(1)}) all-reduce(f32[128]{0:T(128)S(1)} %bitcast_reduce_fusion.1, f32[128]{0:T(128)S(1)} %add.52), channel_id=1, replica_groups=mesh['dp'=4,'group'=8] {'group'}, use_global_device_ids=true, to_apply=%region_17.18 | all-reduce | flops 256 | bytes 2048 | tf_op jit(solution)/shard_map/psum | solution.py:90
  138.9 12.2 %all-reduce.3 = (f32[128]{0:T(128)}, f32[128]{0:T(128)}) all-reduce(f32[128]{0:T(128)S(1)} %get-tuple-element.30, f32[128]{0:T(128)S(1)} %get-tuple-element.31), channel_id=1, replica_groups=mesh['dp'=4,'group'=8] {'dp'}, use_global_device_ids=true, to_apply=%region_18.19 | all-reduce | flops 256 | bytes 2048 | tf_op jit(solution)/shard_map/psum | solution.py:90
  151.1 1.3 fusion.86
  (139 shorter events, 8.8 us)
Async XLA Ops:
  7.2 16.6 %copy-start.14 = (bf16[128,4096]{1,0:T(8,128)(2,1)S(1)}, bf16[128,4096]{1,0:T(8,128)(2,1)}, u32[]{:S(2)}) copy-start(bf16[128,4096]{1,0:T(8,128)(2,1)} %param.9) | copy-start | bytes 3145732
  7.2 118.2 %all-reduce.6.cloned.1.call-start = ((), (), s32[]{:S(2)}) async-start(), calls=%async_computation | async-start | bytes 131072
  8.5 16.2 %copy-start.38 = (f32[512]{0:T(512)}, f32[512]{0:T(512)S(1)}, u32[]{:S(2)}) copy-start(f32[512]{0:T(512)S(1)} %broadcast_bitcast_fusion.3) | copy-start | bytes 6148
  9.2 0.6 copy-start.30
  9.3 0.6 copy-start.40
  9.9 0.6 copy-start.32
  23.5 2.0 %copy-start.36 = (f32[128,4]{0,1:T(4,128)}, f32[128,4]{0,1:T(4,128)S(1)}, u32[]{:S(2)}) copy-start(f32[128,4]{0,1:T(4,128)S(1)} %add_rsqrt_fusion.1) | copy-start | bytes 6148
  24.4 1.5 copy-start
  30.0 3.9 %copy-start.6 = (bf16[128,4,8,128]{3,0,2,1:T(8,128)(2,1)}, bf16[128,4,8,128]{3,0,2,1:T(8,128)(2,1)S(1)}, u32[]{:S(2)}) copy-start(bf16[128,4,8,128]{3,0,2,1:T(8,128)(2,1)S(1)} %multiply_convert_fusion) | copy-start | bytes 3145732
  62.1 3.2 %copy-start.5 = (f32[8,128,160]{1,2,0:T(8,128)S(1)}, f32[8,128,160]{1,2,0:T(8,128)}, u32[]{:S(2)}) copy-start(f32[8,128,160]{1,2,0:T(8,128)} %fusion.50) | copy-start | bytes 1966084
  62.1 4.4 %copy-start.7 = (bf16[128,4,8,128]{3,0,2,1:T(8,128)(2,1)S(1)}, bf16[128,4,8,128]{3,0,2,1:T(8,128)(2,1)}, u32[]{:S(2)}) copy-start(bf16[128,4,8,128]{3,0,2,1:T(8,128)(2,1)} %copy-done.6) | copy-start | bytes 3145732
  62.1 4.6 %copy-start.4 = (f32[8,128,160]{1,2,0:T(8,128)S(1)}, f32[8,128,160]{1,2,0:T(8,128)}, u32[]{:S(2)}) copy-start(f32[8,128,160]{1,2,0:T(8,128)} %fusion.52) | copy-start | bytes 1966084
  63.5 7.1 %copy-start.19 = (bf16[160,1,128]{2,0,1:T(8,128)(2,1)}, bf16[160,1,128]{2,0,1:T(8,128)(2,1)S(1)}, u32[]{:S(2)}) copy-start(bf16[160,1,128]{2,0,1:T(8,128)(2,1)S(1)} %convolution_bitcast_fusion.8) | copy-start | bytes 122884
  63.6 3.4 %copy-start.17 = (bf16[128,1,8,128]{3,0,2,1:T(8,128)(2,1)S(1)}, bf16[128,1,8,128]{3,0,2,1:T(8,128)(2,1)}, u32[]{:S(2)}) copy-start(bf16[128,1,8,128]{3,0,2,1:T(8,128)(2,1)} %copy.137) | copy-start | bytes 786436
  63.6 3.4 %copy-start.29 = (bf16[160,1,128]{2,1,0:T(2,128)(2,1)S(1)}, bf16[160,1,128]{2,1,0:T(2,128)(2,1)}, u32[]{:S(2)}) copy-start(bf16[160,1,128]{2,1,0:T(2,128)(2,1)} %get-tuple-element.45) | copy-start | bytes 122884
  66.4 1.6 copy-start.8
  66.7 1.3 copy-start.3
  67.0 3.7 %copy-start.21 = (bf16[160,1,128]{2,0,1:T(8,128)(2,1)}, bf16[160,1,128]{2,0,1:T(8,128)(2,1)S(1)}, u32[]{:S(2)}) copy-start(bf16[160,1,128]{2,0,1:T(8,128)(2,1)S(1)} %convolution_bitcast_fusion.9) | copy-start | bytes 122884
  67.0 1.4 copy-start.16
  67.0 1.4 copy-start.28
  67.8 1.6 copy-start.9
  68.0 1.3 copy-start.2
  68.3 2.4 %copy-start.23 = (bf16[160,1,128]{2,0,1:T(8,128)(2,1)}, bf16[160,1,128]{2,0,1:T(8,128)(2,1)S(1)}, u32[]{:S(2)}) copy-start(bf16[160,1,128]{2,0,1:T(8,128)(2,1)S(1)} %convolution_bitcast_fusion.10) | copy-start | bytes 122884
  68.3 1.3 copy-start.15
  68.3 1.3 copy-start.27
  69.1 1.6 copy-start.10
  69.6 1.5 copy-start.25
  70.4 0.7 copy-start.12
  70.4 6.5 %copy-start.18 = (bf16[32,4,128]{2,0,1:T(8,128)(2,1)S(1)}, bf16[32,4,128]{2,0,1:T(8,128)(2,1)}, u32[]{:S(2)}) copy-start(bf16[32,4,128]{2,0,1:T(8,128)(2,1)} %copy.94) | copy-start | bytes 98308
  71.1 5.7 %copy-start.11 = (bf16[8,128,160]{1,2,0:T(8,128)(2,1)S(1)}, bf16[8,128,160]{1,2,0:T(8,128)(2,1)}, u32[]{:S(2)}) copy-start(bf16[8,128,160]{1,2,0:T(8,128)(2,1)} %copy-done.10) | copy-start | bytes 983044
  71.1 7.6 %copy-start.13 = (bf16[8,128,160]{1,2,0:T(8,128)(2,1)S(1)}, bf16[8,128,160]{1,2,0:T(8,128)(2,1)}, u32[]{:S(2)}) copy-start(bf16[8,128,160]{1,2,0:T(8,128)(2,1)} %copy-done.12) | copy-start | bytes 983044
  71.8 6.2 %copy-start.20 = (bf16[160,1,128]{2,0,1:T(8,128)(2,1)S(1)}, bf16[160,1,128]{2,0,1:T(8,128)(2,1)}, u32[]{:S(2)}) copy-start(bf16[160,1,128]{2,0,1:T(8,128)(2,1)} %copy-done.19) | copy-start | bytes 122884
  71.8 6.2 %copy-start.22 = (bf16[160,1,128]{2,0,1:T(8,128)(2,1)S(1)}, bf16[160,1,128]{2,0,1:T(8,128)(2,1)}, u32[]{:S(2)}) copy-start(bf16[160,1,128]{2,0,1:T(8,128)(2,1)} %copy-done.21) | copy-start | bytes 122884
  71.8 6.2 %copy-start.24 = (bf16[160,1,128]{2,0,1:T(8,128)(2,1)S(1)}, bf16[160,1,128]{2,0,1:T(8,128)(2,1)}, u32[]{:S(2)}) copy-start(bf16[160,1,128]{2,0,1:T(8,128)(2,1)} %copy-done.23) | copy-start | bytes 122884
  71.8 6.2 %copy-start.26 = (bf16[160,1,128]{2,0,1:T(8,128)(2,1)S(1)}, bf16[160,1,128]{2,0,1:T(8,128)(2,1)}, u32[]{:S(2)}) copy-start(bf16[160,1,128]{2,0,1:T(8,128)(2,1)} %copy-done.25) | copy-start | bytes 122884
  74.7 5.3 %copy-start.37 = (f32[128,4]{0,1:T(4,128)S(1)}, f32[128,4]{0,1:T(4,128)}, u32[]{:S(2)}) copy-start(f32[128,4]{0,1:T(4,128)} %copy-done.36) | copy-start | bytes 6148
  74.7 5.3 %copy-start.42 = (f32[128]{0:T(128)S(1)}, f32[128]{0:T(128)}, u32[]{:S(2)}) copy-start(f32[128]{0:T(128)} %param.16) | copy-start | bytes 1540
  76.9 3.6 %copy-start.43 = (f32[128]{0:T(128)S(1)}, f32[128]{0:T(128)}, u32[]{:S(2)}) copy-start(f32[128]{0:T(128)} %param.15) | copy-start | bytes 1540
  84.1 3.0 %copy-start.1 = (bf16[128,4096]{0,1:T(8,128)(2,1)S(1)}, bf16[128,4096]{0,1:T(8,128)(2,1)}, u32[]{:S(2)}) copy-start(bf16[128,4096]{0,1:T(8,128)(2,1)} %copy-done) | copy-start | bytes 3145732
  84.1 3.0 %copy-start.34 = (f32[128,32]{0,1:T(8,128)S(1)}, f32[128,32]{0,1:T(8,128)}, u32[]{:S(2)}) copy-start(f32[128,32]{0,1:T(8,128)} %get-tuple-element.50) | copy-start | bytes 49156
  87.1 2.7 %copy-start.41 = (f32[4,4]{1,0:T(4,128)S(1)}, f32[4,4]{1,0:T(4,128)}, u32[]{:S(2)}) copy-start(f32[4,4]{1,0:T(4,128)} %copy-done.40) | copy-start | bytes 196
  87.1 2.8 %copy-start.35 = (bf16[4,512]{1,0:T(4,128)(2,1)S(1)}, bf16[4,512]{1,0:T(4,128)(2,1)}, u32[]{:S(2)}) copy-start(bf16[4,512]{1,0:T(4,128)(2,1)} %param.12) | copy-start | bytes 12292
  87.1 2.8 %slice-start = ((bf16[160,4,128]{2,0,1:T(8,128)(2,1)}), bf16[128,4,128]{2,0,1:T(8,128)(2,1)S(1)}, s32[]{:S(2)}) async-start(bf16[160,4,128]{2,0,1:T(8,128)(2,1)} %maximum_convert_fusion), calls=%async_computation.1 | async-start | bytes 262144 | tf_op jit(solution)/shard_map/slice | solution.py:84
  89.7 3.3 %copy-start.44 = (u32[32]{0:T(128)S(1)}, u32[32]{0:T(128)}, u32[]{:S(2)}) copy-start(u32[32]{0:T(128)} %constant.31) | copy-start | bytes 388
  89.7 37.1 %copy-start.31 = (f32[4,4,128]{2,1,0:T(4,128)S(1)}, f32[4,4,128]{2,1,0:T(4,128)}, u32[]{:S(2)}) copy-start(f32[4,4,128]{2,1,0:T(4,128)} %copy-done.30) | copy-start | bytes 24580
  89.8 61.4 %copy-start.33 = (f32[1,4,4,128]{3,2,1,0:T(4,128)S(1)}, f32[1,4,4,128]{3,2,1,0:T(4,128)}, u32[]{:S(2)}) copy-start(f32[1,4,4,128]{3,2,1,0:T(4,128)} %copy-done.32) | copy-start | bytes 24580
  89.8 61.4 %copy-start.39 = (f32[512]{0:T(512)S(1)}, f32[512]{0:T(512)}, u32[]{:S(2)}) copy-start(f32[512]{0:T(512)} %copy-done.38) | copy-start | bytes 6148
Sparse Core Ops, SparseCore 0:
  71.9 53.4 all-reduce.5
